TPU v7x, 32 devices: a whole 2x2x4 slice. The times are simulated.
32 devices in a mesh: req: 8 (over z, x), head: 4 (over y, core).
Axes of the slice: x: 2, y: 2, z: 4, core: 2. Of those that a mesh axis runs over, the one named last changes fastest.
Arguments:
- hidden_state: bfloat16 [64, 2048], P('req'), may hold values from -6 to 6
- attend_gain: float32 [2048], replicated, may hold values from 0.1 to 1.9
- input_weight: bfloat16 [2048, 3, 2048], P(None, None, 'head'), may hold values from -0.125 to 0.125
- input_bias: float32 [3, 2048], P(None, 'head'), may hold values from -3 to 3
- output_weight: bfloat16 [2048, 2048], P('head'), may hold values from -0.125 to 0.125
- window_cache: bfloat16 [64, 2, 2048, 2048], P('req', None, None, 'head'), may hold values from -9 to 9
- sink_cache: bfloat16 [64, 2, 4, 2048], P('req', None, None, 'head'), may hold values from -3000 to 3000
- lengths: int32 [64], P('req'), may hold values from 16 to 32768, as said below
- expert_index: int32 [64, 4], P('req'), may hold values from 0 to 31, all different within a row; in each aligned block of 8 rows (0 to 7, 8 to 15, ...) at most 2 rows name the same one
- router_weight: float32 [64, 4], P('req'), may hold values from 0.05 to 0.5
- mixture_gain: float32 [2048], replicated, may hold values from 0.1 to 1.9
- expert_gate_up: bfloat16 [2, 45056, 2048], P(None, ('req', 'head')), may hold values from -0.125 to 0.125
- expert_down: bfloat16 [45056, 2048], P(('req', 'head')), may hold values from -0.3125 to 0.3125
- shared_gate_up: bfloat16 [2, 2048, 5632], P(None, 'req', 'head'), may hold values from -0.125 to 0.125
- shared_down: bfloat16 [5632, 2048], P('head', 'req'), may hold values from -0.078125 to 0.078125
- shared_gate: float32 [2048], replicated, may hold values from -0.125 to 0.125
Outputs:
- layer_out: bfloat16 [64, 2048], P('req', 'head')
- new_kv: bfloat16 [64, 2, 2048], P('req', None, 'head')
Inputs may be any that keep to these rules, and one draw needn't show every extreme that they name: Request r has lengths[r] cached tokens and its new token takes position lengths[r]; some request has exactly 32768 cached tokens and some has 16. `expert_index`: each row names 4 different experts; within the rows of one index of req (aligned blocks of 8 rows) no expert is named more than 2 times, a bound that some block reaches.
All inputs are finite; a program needn't handle non-finite values.
Results may differ from a plain program's by a relative error of at most 0.014.
The roundings to bfloat16 on the way count: a program that leaves them out, or rounds other values in their place, can miss the bound.
Values may be sent and summed in bfloat16 or wider, within the bound.
No kernel may reach another device: no remote copies, remote signals or barrier semaphores. Data moves between devices by JAX's collectives and lax.ppermute only.
A program may use at most 256 MiB of HBM per device.

v0:
```python
import math
import jax
import jax.numpy as jnp
from jax import lax
from jax.sharding import PartitionSpec as P

HD = 128
EXPERTS = 32
FE = 1408
SINKS = 4
CAP = 2
EPSILON = 1e-06
ROPE_BASE = 1000000.0


def rms_scale(values, gains):
    mean_square = jnp.mean(values * values, axis=-1, keepdims=True)
    return values * lax.rsqrt(mean_square + EPSILON) * gains


def rotate(vectors, positions):
    half_depth = vectors.shape[-1] // 2
    steps_half = jnp.arange(half_depth).astype(jnp.float32)
    frequencies = jnp.float32(ROPE_BASE) ** (-(2.0 / vectors.shape[-1]) * steps_half)
    angles = positions.astype(jnp.float32)[:, None] * frequencies[None, :]
    cosine = jnp.cos(angles)[:, None, :]
    sine_terms = jnp.sin(angles)[:, None, :]
    lower_half = vectors[..., :half_depth]
    upper_half = vectors[..., half_depth:]
    return jnp.concatenate(
        [
            lower_half * cosine - upper_half * sine_terms,
            upper_half * cosine + lower_half * sine_terms,
        ],
        axis=-1,
    )


def block_scores(queries, fresh_key, window_cache, fresh_slot, live_count, block_size):
    row_count, head_count, head_depth = queries.shape
    key_rows = window_cache[:, 0].reshape(row_count, block_size, head_count, head_depth)
    scores = jnp.einsum("rhd,rshd->rhs", queries, key_rows, preferred_element_type=jnp.float32)
    fresh_scores = jnp.einsum("rhd,rhd->rh", queries, fresh_key, preferred_element_type=jnp.float32)
    positions = jnp.arange(block_size)
    is_fresh = positions[None, :] == fresh_slot[:, None]
    scores = jnp.where(is_fresh[:, None, :], fresh_scores[:, :, None], scores) / math.sqrt(
        head_depth
    )
    keeping = positions[None, :] < live_count[:, None]
    return jnp.where(keeping[:, None, :], scores, -jnp.inf)


def block_values(window_cache, block_size, head_count, head_depth):
    row_count = window_cache.shape[0]
    return window_cache[:, 1].reshape(row_count, block_size, head_count, head_depth)


def window_values(weights, is_fresh, value_rows, fresh_value):
    kept_weights = jnp.where(is_fresh[:, None, :], jnp.zeros_like(weights), weights)
    fresh_weight = jnp.sum(
        jnp.where(is_fresh[:, None, :], weights, jnp.zeros_like(weights)), axis=-1
    )
    window_part = jnp.einsum(
        "rhs,rshd->rhd", kept_weights, value_rows, preferred_element_type=jnp.float32
    )
    return window_part + fresh_weight.astype(jnp.float32)[..., None] * fresh_value.astype(
        jnp.float32
    )


def expert_slice(arrived, expert_gate_up, expert_down):
    gate_terms = jnp.einsum(
        "nkd,fd->nkf", arrived, expert_gate_up[0], preferred_element_type=jnp.float32
    )
    up_terms = jnp.einsum(
        "nkd,fd->nkf", arrived, expert_gate_up[1], preferred_element_type=jnp.float32
    )
    hidden_units = (jax.nn.silu(gate_terms) * up_terms).astype(jnp.bfloat16)
    return jnp.einsum("nkf,fd->nkd", hidden_units, expert_down, preferred_element_type=jnp.float32)


def local(
    hidden_state,
    attend_gain,
    input_weight,
    input_bias,
    output_weight,
    window_cache,
    sink_cache,
    lengths,
    expert_index,
    router_weight,
    mixture_gain,
    expert_gate_up,
    expert_down,
    shared_gate_up,
    shared_down,
    shared_gate,
):
    row_count, model_width = hidden_state.shape
    local_width = input_weight.shape[2]
    head_depth = HD
    head_count = local_width // head_depth
    window_length = window_cache.shape[2]
    normed = rms_scale(hidden_state.astype(jnp.float32), attend_gain).astype(jnp.bfloat16)
    projected = jnp.dot(
        normed,
        input_weight.reshape(model_width, 3 * local_width),
        preferred_element_type=jnp.float32,
    ) + input_bias.reshape(3 * local_width)
    projected = projected.reshape(row_count, 3, head_count, head_depth)
    queries = rotate(projected[:, 0], lengths).astype(jnp.bfloat16)
    fresh_key = rotate(projected[:, 1], lengths).astype(jnp.bfloat16)
    fresh_value = projected[:, 2].astype(jnp.bfloat16)
    new_kv = jnp.stack(
        [fresh_key.reshape(row_count, local_width), fresh_value.reshape(row_count, local_width)],
        axis=1,
    )
    fresh_slot = (lengths - SINKS) % window_length
    live_count = jnp.minimum(lengths - SINKS + 1, window_length)
    sink_keys = sink_cache[:, 0].reshape(row_count, SINKS, head_count, head_depth)
    sink_values = sink_cache[:, 1].reshape(row_count, SINKS, head_count, head_depth)
    sink_scores = jnp.einsum(
        "rhd,rshd->rhs", queries, sink_keys, preferred_element_type=jnp.float32
    ) / math.sqrt(head_depth)
    scores = block_scores(queries, fresh_key, window_cache, fresh_slot, live_count, window_length)
    is_fresh = jnp.arange(window_length)[None, :] == fresh_slot[:, None]
    value_rows = block_values(window_cache, window_length, head_count, head_depth)
    score_peak = jnp.maximum(jnp.max(sink_scores, axis=-1), jnp.max(scores, axis=-1))
    window_exp = jnp.exp(scores - score_peak[..., None])
    score_total = jnp.sum(jnp.exp(sink_scores - score_peak[..., None]), axis=-1) + jnp.sum(
        window_exp, axis=-1
    )
    weights = (window_exp / score_total[..., None]).astype(jnp.bfloat16)
    accum = window_values(weights, is_fresh, value_rows, fresh_value)
    sink_weights = (jnp.exp(sink_scores - score_peak[..., None]) / score_total[..., None]).astype(
        jnp.bfloat16
    )
    accum = accum + jnp.einsum(
        "rhs,rshd->rhd", sink_weights, sink_values, preferred_element_type=jnp.float32
    )
    attended = accum.astype(jnp.bfloat16).reshape(row_count, local_width)
    attend_part = jnp.dot(attended, output_weight, preferred_element_type=jnp.float32)
    resid = hidden_state.astype(jnp.float32) + lax.psum(attend_part, "head")
    tokens = rms_scale(resid, mixture_gain).astype(jnp.bfloat16)
    all_tokens = lax.all_gather(tokens, "req", axis=0, tiled=True)
    group_index = lax.axis_index("req")
    group_count = lax.axis_size("req")
    row_width = shared_gate_up.shape[1]
    my_columns = lax.dynamic_slice_in_dim(all_tokens, group_index * row_width, row_width, 1)
    shared_terms = jnp.einsum(
        "td,cdf->ctf", my_columns, shared_gate_up, preferred_element_type=jnp.float32
    )
    shared_terms = lax.psum(shared_terms, "req")
    shared_hidden = (jax.nn.silu(shared_terms[0]) * shared_terms[1]).astype(jnp.bfloat16)
    gate_value = jax.nn.sigmoid(
        jnp.dot(all_tokens.astype(jnp.float32), shared_gate, precision=lax.Precision.HIGHEST)
    )
    shared_out = gate_value[:, None] * jnp.dot(
        shared_hidden, shared_down, preferred_element_type=jnp.float32
    )
    expert_hot = (expert_index[:, :, None] == jnp.arange(EXPERTS)[None, None, :]).astype(
        jnp.float32
    )
    combine = jnp.sum(expert_hot * router_weight[:, :, None], axis=1)
    local_experts = EXPERTS // group_count
    quarters = FE // expert_down.shape[0]
    local_pick = lax.axis_index("head") // quarters
    expert_hit = jnp.sum(expert_hot, axis=1)
    slot_rank = jnp.cumsum(expert_hit, axis=0) - expert_hit
    chosen = expert_hit[:, :, None] * (
        slot_rank[:, :, None] == jnp.arange(CAP)[None, None, :]
    ).astype(jnp.float32)
    mine_hot = (jnp.arange(local_experts) == local_pick).astype(jnp.float32)
    chosen_mine = jnp.einsum(
        "rglc,l->rgc",
        chosen.reshape(row_count, group_count, local_experts, CAP),
        mine_hot,
        precision=lax.Precision.HIGHEST,
    )
    combine_mine = jnp.einsum(
        "rgl,l->rg",
        combine.reshape(row_count, group_count, local_experts),
        mine_hot,
        precision=lax.Precision.HIGHEST,
    )
    placing = chosen_mine.reshape(row_count, group_count * CAP)
    outgoing = jnp.dot(
        placing.T.astype(jnp.bfloat16), tokens, preferred_element_type=jnp.float32
    ).astype(jnp.bfloat16)
    outgoing = outgoing.reshape(group_count, CAP, model_width)
    produced = expert_slice(
        lax.all_to_all(outgoing, "req", split_axis=0, concat_axis=0, tiled=True),
        expert_gate_up,
        expert_down,
    )
    returned = lax.all_to_all(produced, "req", split_axis=0, concat_axis=0, tiled=True)
    weighting = (chosen_mine * combine_mine[:, :, None]).reshape(row_count, group_count * CAP)
    routed = jnp.dot(
        weighting,
        returned.reshape(group_count * CAP, model_width),
        precision=lax.Precision.HIGHEST,
        preferred_element_type=jnp.float32,
    )
    routed = routed + lax.all_to_all(shared_out, "req", split_axis=0, concat_axis=1, tiled=True)
    final = lax.psum_scatter(routed, "head", scatter_dimension=1, tiled=True)
    slice_width = final.shape[1]
    own_resid = lax.dynamic_slice_in_dim(
        resid, lax.axis_index("head") * slice_width, slice_width, 1
    )
    return ((own_resid + final).astype(jnp.bfloat16), new_kv)


def solution(mesh):
    return jax.shard_map(
        local,
        mesh=mesh,
        in_specs=(
            P("req", None),
            P(),
            P(None, None, "head"),
            P(None, "head"),
            P("head", None),
            P("req", None, None, "head"),
            P("req", None, None, "head"),
            P("req"),
            P("req", None),
            P("req", None),
            P(),
            P(None, ("req", "head"), None),
            P(("req", "head"), None),
            P(None, "req", "head"),
            P("head", "req"),
            P(),
        ),
        out_specs=(P("req", "head"), P("req", None, "head")),
        check_vma=False,
    )
```

profile of v0, /device:TPU:0, one launch (start us, length us, event | category | flops | bytes accessed | tf_op | source)
XLA Modules:
  0.0 306.4 jit_solution(18246826656507924227)
XLA Ops:
  8.1 8.8 %copy.43 = bf16[2048,3,512]{0,2,1:T(8,128)(2,1)} copy(bf16[2048,3,512]{2,0,1:T(8,128)(2,1)} %param.18) | data formatting | bytes 12582912 | tf_op args[2]
  17.1 4.5 %convolution_add_fusion = f32[8,1536]{1,0:T(8,128)S(1)} fusion(bf16[2048,1536]{0,1:T(8,128)(2,1)} %bitcast.145, bf16[8,2048]{1,0:T(8,128)(2,1)S(1)} %copy-done.4, f32[2048]{0:T(1024)S(1)} %copy-done.7, f32[8]{0:T(128)S(1)} %add_rsqrt_fusion.1, f32[1536]{0:T(1024)S(1)} %add.96), kind=kOutput, calls=%fused_computation.14 | convolution fusion | flops 50409472 | bytes 6387744 | tf_op jit(solution)/shard_map/dot_general | solution.py:106
  22.5 22.5 %fusion.80 = (bf16[8,1,2048,512]{3,2,1,0:T(8,128)(2,1)}, bf16[8,1,2048,512]{3,2,1,0:T(8,128)(2,1)}) fusion(bf16[8,2,2048,512]{3,2,1,0:T(8,128)(2,1)} %param.21), kind=kLoop, calls=%fused_computation.124 | loop fusion | bytes 67108864 | tf_op jit(solution)/shard_map/slice | solution.py:55
  45.0 21.6 %copy.77 = bf16[8,1,2048,512]{2,3,0,1:T(8,128)(2,1)} copy(bf16[8,1,2048,512]{3,2,1,0:T(8,128)(2,1)} %get-tuple-element.17) | data formatting | bytes 33554432 | tf_op jit(solution)/shard_map/reshape;squeeze | solution.py:41
  66.7 8.0 %fusion.58 = f32[8,4,1,2048]{3,2,1,0:T(1,128)S(1)} fusion(bf16[8,2048,4,128]{1,3,2,0:T(8,128)(2,1)} %bitcast.144, bf16[8,4,128,1]{2,0,1,3:T(8,128)(2,1)S(1)} %fusion.72), kind=kOutput, calls=%fused_computation.87 | convolution fusion | flops 16777216 | bytes 17047552 | tf_op jit(solution)/shard_map/rhd,rshd->rhs/dot_general | solution.py:42
  77.5 23.7 %reshape_squeeze.14 = bf16[8,2048,4,128]{3,2,1,0:T(4,128)(2,1)} reshape(bf16[8,1,2048,512]{3,2,1,0:T(8,128)(2,1)} %get-tuple-element.16) | data formatting | bytes 33554432 | tf_op jit(solution)/shard_map/reshape;squeeze | solution.py:55
  101.4 8.3 %fusion = f32[8,4,1,128]{3,2,1,0:T(1,128)S(1)} fusion(bf16[8,2048,4,128]{3,2,1,0:T(4,128)(2,1)} %reshape_squeeze.14, bf16[8,4,2048,1]{2,0,1,3:T(8,128)(2,1)} %select_bitcast_fusion), kind=kOutput, calls=%fused_computation | convolution fusion | flops 16777216 | bytes 16924672 | tf_op jit(solution)/shard_map/rhs,rshd->rhd/dot_general | solution.py:63
  109.8 1.8 fusion.61
  114.3 3.2 %reduce_window_sum.14 = f32[8,8,4]{0,2,1:T(4,128)} reduce-window(f32[8,8,4]{0,2,1:T(4,128)S(1)} %bitcast.147, f32[]{:T(128)} %constant.67.clone.1), window={size=8x1x1 pad=7_0x0_0x0_0}, to_apply=%region_8.9 | reduce-window | flops 1792 | bytes 2052 | tf_op jit(solution)/shard_map/jit(cumsum)/reduce_window_sum | solution.py:170
  118.8 1.4 copy.45
  120.2 1.6 multiply_reduce_fusion
  121.8 1.5 copy.74
  124.9 20.5 %all-reduce.3.cloned.1.call-done = f32[8,2048]{1,0:T(8,128)} async-done(((f32[8,2048]{1,0:T(8,128)}), f32[8,2048]{1,0:T(8,128)}) %all-reduce.3.cloned.1.call-update) | async-done | bytes 65552 | tf_op jit(solution)/shard_map/psum | solution.py:144
  147.8 32.8 %all_gather.3 = bf16[64,2048]{1,0:T(8,128)(2,1)} all-gather(bf16[8,2048]{1,0:T(8,128)(2,1)S(1)} %multiply_convert_fusion), channel_id=1, replica_groups=mesh['req'=8,'head'=4] {'req'}, dimensions={0}, use_global_device_ids=true | all-gather | bytes 294912 | tf_op jit(solution)/shard_map/all_gather | solution.py:146
  181.4 1.5 reshape.198
  182.9 5.4 %all-to-all-start = ((bf16[8,2,2048]{2,1,0:T(2,128)(2,1)}), bf16[8,2,2048]{2,1,0:T(2,128)(2,1)}, u32[]{:S(2)}, u32[]{:S(2)}) async-start(bf16[8,2,2048]{2,1,0:T(2,128)(2,1)} %reshape.198), calls=%async_computation | async-start | bytes 131072 | tf_op jit(solution)/shard_map/all_to_all | solution.py:193
  188.6 2.0 convolution_bitcast_fusion
  190.6 4.7 %all-to-all-done = bf16[8,2,2048]{2,1,0:T(2,128)(2,1)} async-done(((bf16[8,2,2048]{2,1,0:T(2,128)(2,1)}), bf16[8,2,2048]{2,1,0:T(2,128)(2,1)}, u32[]{:S(2)}, u32[]{:S(2)}) %all-to-all-start) | async-done | bytes 65568 | tf_op jit(solution)/shard_map/all_to_all | solution.py:193
  195.3 4.3 %fusion.6 = f32[8,2,1408]{2,0,1:T(8,128)S(1)} fusion(bf16[2,1408,2048]{2,1,0:T(8,128)(2,1)} %param.27, bf16[8,2,2048]{2,1,0:T(2,128)(2,1)} %all-to-all-done), kind=kOutput, calls=%fused_computation.6 | convolution fusion | flops 92274688 | bytes 5922816 | tf_op jit(solution)/shard_map/nkd,fd->nkf/dot_general | solution.py:72
  199.6 7.1 %fusion.2 = f32[8,2,2048]{2,0,1:T(8,128)S(1)} fusion(bf16[1408,2048]{1,0:T(8,128)(2,1)} %param.28, bf16[2,1408,2048]{2,1,0:T(8,128)(2,1)} %param.27, f32[8,2,1408]{2,0,1:T(8,128)S(1)} %fusion.6, bf16[8,2,2048]{2,1,0:T(2,128)(2,1)} %all-to-all-done), kind=kOutput, calls=%fused_computation.2 | convolution fusion | flops 184684544 | bytes 11821056 | tf_op jit(solution)/shard_map/nkf,fd->nkd/dot_general | solution.py:79
  207.4 3.4 %all-to-all-start.1 = ((f32[8,2,2048]{2,1,0:T(2,128)}), f32[8,2,2048]{2,1,0:T(2,128)S(1)}, u32[]{:S(2)}, u32[]{:S(2)}) async-start(f32[8,2,2048]{2,1,0:T(2,128)} %copy.50), calls=%async_computation.1 | async-start | bytes 262144 | tf_op jit(solution)/shard_map/all_to_all | solution.py:197
  211.2 57.6 %all-reduce.5.cloned.1.call-done = f32[2,64,1408]{2,1,0:T(8,128)} async-done(((f32[2,64,1408]{2,1,0:T(8,128)}), f32[2,64,1408]{2,1,0:T(8,128)}) %all-reduce.5.cloned.1.call-update) | async-done | bytes 720912 | tf_op jit(solution)/shard_map/psum | solution.py:154
  270.1 10.4 %all_to_all.29 = f32[8,8,256]{2,1,0:T(8,128)S(1)} all-to-all(f32[8,8,256]{2,1,0:T(8,128)S(1)} %fusion.17), channel_id=1, replica_groups=mesh['req'=8,'head'=4] {'req'}, dimensions={0} | all-to-all | bytes 131072 | tf_op jit(solution)/shard_map/all_to_all | solution.py:205
  282.8 15.7 %reduce-scatter.2.cloned.1.call-done = f32[8,512]{1,0:T(8,128)} async-done(((f32[8,2048]{1,0:T(8,128)}), f32[8,512]{1,0:T(8,128)}) %reduce-scatter.2.cloned.1.call-update) | async-done | bytes 16400 | tf_op jit(solution)/shard_map/reduce_scatter | solution.py:206
  (82 shorter events, 20.1 us)
Async XLA Ops:
  7.2 102.6 %copy-start = (bf16[512,2048]{1,0:T(8,128)(2,1)S(1)}, bf16[512,2048]{1,0:T(8,128)(2,1)}, u32[]{:S(2)}) copy-start(bf16[512,2048]{1,0:T(8,128)(2,1)} %param.20) | copy-start | bytes 6291460
  7.2 9.7 %copy-start.8 = (f32[3,512]{1,0:T(4,128)S(1)}, f32[3,512]{1,0:T(4,128)}, u32[]{:S(2)}) copy-start(f32[3,512]{1,0:T(4,128)} %param.19) | copy-start | bytes 18436
  7.2 9.7 %copy-start.4 = (bf16[8,2048]{1,0:T(8,128)(2,1)S(1)}, bf16[8,2048]{1,0:T(8,128)(2,1)}, u32[]{:S(2)}) copy-start(bf16[8,2048]{1,0:T(8,128)(2,1)} %param.16) | copy-start | bytes 98308
  7.2 9.9 %copy-start.7 = (f32[2048]{0:T(1024)S(1)}, f32[2048]{0:T(1024)}, u32[]{:S(2)}) copy-start(f32[2048]{0:T(1024)} %param.17) | copy-start | bytes 24580
  7.2 138.2 %all-reduce.3.cloned.1.call-start = ((), (), s32[]{:S(2)}) async-start(), calls=%async_computation.4 | async-start | bytes 131072 | tf_op jit(solution)/shard_map/psum | solution.py:144
  21.6 0.6 copy-start.5
  66.6 8.1 %copy-start.12 = (bf16[8,2,4,512]{3,2,1,0:T(4,128)(2,1)S(1)}, bf16[8,2,4,512]{3,2,1,0:T(4,128)(2,1)}, u32[]{:S(2)}) copy-start(bf16[8,2,4,512]{3,2,1,0:T(4,128)(2,1)} %param.22) | copy-start | bytes 196612
  101.4 10.7 %copy-start.9 = (f32[8,4]{0,1:T(4,128)S(1)}, f32[8,4]{0,1:T(4,128)}, u32[]{:S(2)}) copy-start(f32[8,4]{0,1:T(4,128)} %param.25) | copy-start | bytes 388
  101.4 10.7 %copy-start.10 = (s32[8,4]{0,1:T(4,128)S(1)}, s32[8,4]{0,1:T(4,128)}, u32[]{:S(2)}) copy-start(s32[8,4]{0,1:T(4,128)} %param.24) | copy-start | bytes 388
  101.4 87.1 %copy-start.1 = (bf16[2,256,1408]{2,1,0:T(8,128)(2,1)S(1)}, bf16[2,256,1408]{2,1,0:T(8,128)(2,1)}, u32[]{:S(2)}) copy-start(bf16[2,256,1408]{2,1,0:T(8,128)(2,1)} %param.29) | copy-start | bytes 4325380
  146.4 0.6 copy-start.3
  182.9 12.4 %all-to-all-start = ((bf16[8,2,2048]{2,1,0:T(2,128)(2,1)}), bf16[8,2,2048]{2,1,0:T(2,128)(2,1)}, u32[]{:S(2)}, u32[]{:S(2)}) async-start(bf16[8,2,2048]{2,1,0:T(2,128)(2,1)} %reshape.198), calls=%async_computation | async-start | bytes 131072 | tf_op jit(solution)/shard_map/all_to_all | solution.py:193
  188.3 80.4 %all-reduce.5.cloned.1.call-start = ((), (), s32[]{:S(2)}) async-start(), calls=%async_computation.5 | async-start | bytes 1441792 | tf_op jit(solution)/shard_map/psum | solution.py:154
  190.6 20.3 %copy-start.2 = (bf16[64,2048]{1,0:T(8,128)(2,1)S(1)}, bf16[64,2048]{1,0:T(8,128)(2,1)}, u32[]{:S(2)}) copy-start(bf16[64,2048]{1,0:T(8,128)(2,1)} %all_gather.3) | copy-start | bytes 786436
  190.6 20.3 %copy-start.13 = (f32[2048]{0:T(1024)S(1)}, f32[2048]{0:T(1024)}, u32[]{:S(2)}) copy-start(f32[2048]{0:T(1024)} %param.31) | copy-start | bytes 24580
  190.6 78.1 %copy-start.11 = (bf16[1408,256]{1,0:T(8,128)(2,1)S(1)}, bf16[1408,256]{1,0:T(8,128)(2,1)}, u32[]{:S(2)}) copy-start(bf16[1408,256]{1,0:T(8,128)(2,1)} %param.30) | copy-start | bytes 2162692
  190.6 91.5 %copy-start.6 = (bf16[8,4,128]{2,0,1:T(8,128)(2,1)S(1)}, bf16[8,4,128]{2,0,1:T(8,128)(2,1)}, u32[]{:S(2)}) copy-start(bf16[8,4,128]{2,0,1:T(8,128)(2,1)} %get-tuple-element.15) | copy-start | bytes 24580
  207.4 62.7 %all-to-all-start.1 = ((f32[8,2,2048]{2,1,0:T(2,128)}), f32[8,2,2048]{2,1,0:T(2,128)S(1)}, u32[]{:S(2)}, u32[]{:S(2)}) async-start(f32[8,2,2048]{2,1,0:T(2,128)} %copy.50), calls=%async_computation.1 | async-start | bytes 262144 | tf_op jit(solution)/shard_map/all_to_all | solution.py:197
  210.8 87.7 %reduce-scatter.2.cloned.1.call-start = ((), (), s32[]{:S(2)}) async-start(), calls=%async_computation.6 | async-start | bytes 81920 | tf_op jit(solution)/shard_map/reduce_scatter | solution.py:206
Sparse Core Ops, SparseCore 0:
  111.7 33.7 all-reduce.2
  193.1 75.6 all-reduce.4
  281.6 16.9 reduce-scatter.1
where the time goes:
time: 309 us; the launch traced here: 306 us
  waiting for transfers between devices  98.6 us (32%)
  local copies, waits for them, and re-layouts  86.9 us (28%)
  blocking collectives  43.2 us (14%)
  matrix products  39.7 us (13%)
  other arithmetic  14.9 us (5%)
  between operations  14 us (5%)
  starting transfers between devices  9.11 us (3%)
    psum x1, waiting for transfers between devices, local(): shared_terms = lax.psum(shared_terms, 'req')  57.6 us
    all_gather x1, blocking collectives, local(): all_tokens = lax.all_gather(tokens, 'req', axis=0, tiled=True)  32.8 us
    another operation x1, local copies, waits for them, and re-layouts, block_values(): window_cache[:, 1].reshape(row_count, block_size, head_count, head_depth)  23.7 us
    slice x1, local copies, waits for them, and re-layouts, block_values(): window_cache[:, 1].reshape(row_count, block_size, head_count, head_depth)  22.5 us
    another operation x1, local copies, waits for them, and re-layouts, block_scores(): window_cache[:, 0].reshape(row_count, block_size, head_count, head_depth)  21.6 us
    psum x1, waiting for transfers between devices, local(): resid = hidden_state.astype(jnp.float32) + lax.psum(attend_part, 'head')  20.5 us
    reduce_scatter x1, waiting for transfers between devices, local(): final = lax.psum_scatter(routed, 'head', scatter_dimension=1, tiled=True)  15.7 us
    unnamed x30, local copies, waits for them, and re-layouts  10.8 us
  transfers between devices with their start and end apart: 5, of which 4 were waited for; matrix products, arithmetic and copies ran while one was open for 10% of the time, Pallas kernels for 0%

commit v1 on v0

--- a/solution.py
+++ b/solution.py
@@ -11,6 +11,18 @@
 CAP = 2
 EPSILON = 1e-06
 ROPE_BASE = 1000000.0
+
+
+def doubled_up(value, axis, dim):
+    ways, here = (lax.axis_size(axis), lax.axis_index(axis))
+    grown, reach = (value, 1)
+    while reach < ways:
+        theirs = lax.ppermute(grown, axis, [(d, d ^ reach) for d in range(ways)])
+        mine_first = jnp.concatenate([grown, theirs], axis=dim)
+        theirs_first = jnp.concatenate([theirs, grown], axis=dim)
+        grown = jnp.where(here & reach == 0, mine_first, theirs_first)
+        reach = 2 * reach
+    return grown
 
 
 def rms_scale(values, gains):
@@ -143,7 +155,7 @@
     attend_part = jnp.dot(attended, output_weight, preferred_element_type=jnp.float32)
     resid = hidden_state.astype(jnp.float32) + lax.psum(attend_part, "head")
     tokens = rms_scale(resid, mixture_gain).astype(jnp.bfloat16)
-    all_tokens = lax.all_gather(tokens, "req", axis=0, tiled=True)
+    all_tokens = doubled_up(tokens, "req", 0)
     group_index = lax.axis_index("req")
     group_count = lax.axis_size("req")
     row_width = shared_gate_up.shape[1]

time: 309 us -> 293 us (0.948)
  blocking collectives: 43.2 us -> 10.4 us
  other arithmetic: 14.9 us -> 20.1 us
  starting transfers between devices: 9.11 us -> 14.1 us
  waiting for transfers between devices: 98.6 us -> 102 us
  matrix products: 39.7 us -> 42.9 us
    all_gather x1 -> x0, blocking collectives: 32.8 us -> none  [local(): all_tokens = lax.all_gather(tokens, 'req', axis=0, tiled=True)]
    ppermute x0 -> x3, starting transfers between devices: none -> 5.65 us  [doubled_up(): theirs = lax.ppermute(grown, axis, [(d, d ^ reach) for d in range(ways)])]
    select_n x0 -> x3, other arithmetic: none -> 4.25 us  [doubled_up(): grown = jnp.where(here & reach == 0, mine_first, theirs_first)]
    psum x1, waiting for transfers between devices: 57.6 us -> 61.2 us  [local(): shared_terms = lax.psum(shared_terms, 'req')]
  transfers between devices with their start and end apart: 5 -> 8, of which waited for: 4 -> 5; matrix products, arithmetic and copies ran while one was open for 10% -> 12% of each run, Pallas kernels for 0% -> 0%
where the time goes in v1:
time: 293 us; the launch traced here: 290 us
  waiting for transfers between devices  102 us (35%)
  local copies, waits for them, and re-layouts  87 us (30%)
  matrix products  42.9 us (15%)
  other arithmetic  20.1 us (7%)
  starting transfers between devices  14.1 us (5%)
  between operations  14 us (5%)
  blocking collectives  10.4 us (4%)
    psum x1, waiting for transfers between devices, local(): shared_terms = lax.psum(shared_terms, 'req')  61.2 us
    another operation x1, local copies, waits for them, and re-layouts, block_values(): window_cache[:, 1].reshape(row_count, block_size, head_count, head_depth)  23.7 us
    slice x1, local copies, waits for them, and re-layouts, block_values(): window_cache[:, 1].reshape(row_count, block_size, head_count, head_depth)  22.5 us
    another operation x1, local copies, waits for them, and re-layouts, block_scores(): window_cache[:, 0].reshape(row_count, block_size, head_count, head_depth)  21.6 us
    psum x1, waiting for transfers between devices, local(): resid = hidden_state.astype(jnp.float32) + lax.psum(attend_part, 'head')  20.8 us
    reduce_scatter x1, waiting for transfers between devices, local(): final = lax.psum_scatter(routed, 'head', scatter_dimension=1, tiled=True)  15.7 us
    unnamed x30, local copies, waits for them, and re-layouts  11.4 us
    all_to_all x1, blocking collectives, local(): lax.all_to_all(shared_out, 'req', split_axis=0, concat_axis=1, tiled=True)  10.4 us
  transfers between devices with their start and end apart: 8, of which 5 were waited for; matrix products, arithmetic and copies ran while one was open for 12% of the time, Pallas kernels for 0%

profile of v1, /device:TPU:0, one launch (start us, length us, event | category | flops | bytes accessed | tf_op | source)
XLA Modules:
  0.0 290.2 jit_solution(14965054002167410368)
XLA Ops:
  8.1 8.8 %copy.43 = bf16[2048,3,512]{0,2,1:T(8,128)(2,1)} copy(bf16[2048,3,512]{2,0,1:T(8,128)(2,1)} %param.18) | data formatting | bytes 12582912 | tf_op args[2]
  17.1 4.5 %convolution_add_fusion = f32[8,1536]{1,0:T(8,128)S(1)} fusion(bf16[2048,1536]{0,1:T(8,128)(2,1)} %bitcast.145, bf16[8,2048]{1,0:T(8,128)(2,1)S(1)} %copy-done.5, f32[2048]{0:T(1024)S(1)} %copy-done.8, f32[8]{0:T(128)S(1)} %add_rsqrt_fusion.1, f32[1536]{0:T(1024)S(1)} %add.96), kind=kOutput, calls=%fused_computation.14 | convolution fusion | flops 50409472 | bytes 6387744 | tf_op jit(solution)/shard_map/dot_general | solution.py:118
  22.5 22.5 %fusion.80 = (bf16[8,1,2048,512]{3,2,1,0:T(8,128)(2,1)}, bf16[8,1,2048,512]{3,2,1,0:T(8,128)(2,1)}) fusion(bf16[8,2,2048,512]{3,2,1,0:T(8,128)(2,1)} %param.21), kind=kLoop, calls=%fused_computation.127 | loop fusion | bytes 67108864 | tf_op jit(solution)/shard_map/slice | solution.py:67
  45.0 21.6 %copy.77 = bf16[8,1,2048,512]{2,3,0,1:T(8,128)(2,1)} copy(bf16[8,1,2048,512]{3,2,1,0:T(8,128)(2,1)} %get-tuple-element.17) | data formatting | bytes 33554432 | tf_op jit(solution)/shard_map/reshape;squeeze | solution.py:53
  66.7 8.0 %fusion.58 = f32[8,4,1,2048]{3,2,1,0:T(1,128)S(1)} fusion(bf16[8,2048,4,128]{1,3,2,0:T(8,128)(2,1)} %bitcast.144, bf16[8,4,128,1]{2,0,1,3:T(8,128)(2,1)S(1)} %fusion.72), kind=kOutput, calls=%fused_computation.90 | convolution fusion | flops 16777216 | bytes 17047552 | tf_op jit(solution)/shard_map/rhd,rshd->rhs/dot_general | solution.py:54
  76.8 23.7 %reshape_squeeze.14 = bf16[8,2048,4,128]{3,2,1,0:T(4,128)(2,1)} reshape(bf16[8,1,2048,512]{3,2,1,0:T(8,128)(2,1)} %get-tuple-element.16) | data formatting | bytes 33554432 | tf_op jit(solution)/shard_map/reshape;squeeze | solution.py:67
  100.8 9.2 %fusion = f32[8,4,1,128]{3,2,1,0:T(1,128)S(1)} fusion(bf16[8,2048,4,128]{3,2,1,0:T(4,128)(2,1)} %reshape_squeeze.14, bf16[8,4,2048,1]{2,0,1,3:T(8,128)(2,1)S(1)} %select_bitcast_fusion), kind=kOutput, calls=%fused_computation | convolution fusion | flops 16777216 | bytes 16924672 | tf_op jit(solution)/shard_map/rhs,rshd->rhd/dot_general | solution.py:75
  110.0 1.9 fusion.61
  114.6 3.2 %reduce_window_sum.14 = f32[8,8,4]{0,2,1:T(4,128)} reduce-window(f32[8,8,4]{0,2,1:T(4,128)S(1)} %bitcast.147, f32[]{:T(128)} %constant.69.clone.1), window={size=8x1x1 pad=7_0x0_0x0_0}, to_apply=%region_8.9 | reduce-window | flops 1792 | bytes 2052 | tf_op jit(solution)/shard_map/jit(cumsum)/reduce_window_sum | solution.py:182
  122.6 1.6 multiply_reduce_fusion
  125.1 20.8 %all-reduce.3.cloned.1.call-done = f32[8,2048]{1,0:T(8,128)} async-done(((f32[8,2048]{1,0:T(8,128)}), f32[8,2048]{1,0:T(8,128)}) %all-reduce.3.cloned.1.call-update) | async-done | bytes 65552 | tf_op jit(solution)/shard_map/psum | solution.py:156
  154.5 1.5 collective-permute-start.1
  156.0 1.5 convolution_convert_fusion
  157.5 1.5 reshape.198
  159.0 4.6 %all-to-all-start = ((bf16[8,2,2048]{2,1,0:T(2,128)(2,1)}), bf16[8,2,2048]{2,1,0:T(2,128)(2,1)}, u32[]{:S(2)}, u32[]{:S(2)}) async-start(bf16[8,2,2048]{2,1,0:T(2,128)(2,1)} %reshape.198), calls=%async_computation | async-start | bytes 131072 | tf_op jit(solution)/shard_map/all_to_all | solution.py:205
  163.8 1.6 maximum_select_fusion.1
  165.5 2.7 collective-permute-start.2
  168.2 2.5 all-to-all-done
  170.6 4.9 %fusion.6 = f32[8,2,1408]{2,0,1:T(8,128)} fusion(bf16[2,1408,2048]{2,1,0:T(8,128)(2,1)} %param.27, bf16[8,2,2048]{2,1,0:T(2,128)(2,1)} %all-to-all-done), kind=kOutput, calls=%fused_computation.6 | convolution fusion | flops 92274688 | bytes 5922816 | tf_op jit(solution)/shard_map/nkd,fd->nkf/dot_general | solution.py:84
  178.7 7.3 %fusion.2 = f32[8,2,2048]{2,0,1:T(8,128)S(1)} fusion(bf16[1408,2048]{1,0:T(8,128)(2,1)} %param.28, bf16[2,1408,2048]{2,1,0:T(8,128)(2,1)} %param.27, f32[8,2,1408]{2,0,1:T(8,128)} %fusion.6, bf16[8,2,2048]{2,1,0:T(2,128)(2,1)} %all-to-all-done), kind=kOutput, calls=%fused_computation.2 | convolution fusion | flops 184684544 | bytes 11821056 | tf_op jit(solution)/shard_map/nkf,fd->nkd/dot_general | solution.py:91
  186.7 3.5 %all-to-all-start.1 = ((f32[8,2,2048]{2,1,0:T(2,128)}), f32[8,2,2048]{2,1,0:T(2,128)S(1)}, u32[]{:S(2)}, u32[]{:S(2)}) async-start(f32[8,2,2048]{2,1,0:T(2,128)} %copy.50), calls=%async_computation.1 | async-start | bytes 262144 | tf_op jit(solution)/shard_map/all_to_all | solution.py:209
  191.3 61.2 %all-reduce.5.cloned.1.call-done = f32[2,64,1408]{2,1,0:T(8,128)} async-done(((f32[2,64,1408]{2,1,0:T(8,128)}), f32[2,64,1408]{2,1,0:T(8,128)}) %all-reduce.5.cloned.1.call-update) | async-done | bytes 720912 | tf_op jit(solution)/shard_map/psum | solution.py:166
  253.9 10.4 %all_to_all.29 = f32[8,8,256]{2,1,0:T(8,128)S(1)} all-to-all(f32[8,8,256]{2,1,0:T(8,128)S(1)} %fusion.17), channel_id=1, replica_groups=mesh['req'=8,'head'=4] {'req'}, dimensions={0} | all-to-all | bytes 131072 | tf_op jit(solution)/shard_map/all_to_all | solution.py:217
  266.6 15.7 %reduce-scatter.2.cloned.1.call-done = f32[8,512]{1,0:T(8,128)} async-done(((f32[8,2048]{1,0:T(8,128)}), f32[8,512]{1,0:T(8,128)}) %reduce-scatter.2.cloned.1.call-update) | async-done | bytes 16400 | tf_op jit(solution)/shard_map/reduce_scatter | solution.py:218
  (90 shorter events, 31.4 us)
Async XLA Ops:
  7.2 102.9 %copy-start = (bf16[512,2048]{1,0:T(8,128)(2,1)S(1)}, bf16[512,2048]{1,0:T(8,128)(2,1)}, u32[]{:S(2)}) copy-start(bf16[512,2048]{1,0:T(8,128)(2,1)} %param.20) | copy-start | bytes 6291460
  7.2 9.7 %copy-start.9 = (f32[3,512]{1,0:T(4,128)S(1)}, f32[3,512]{1,0:T(4,128)}, u32[]{:S(2)}) copy-start(f32[3,512]{1,0:T(4,128)} %param.19) | copy-start | bytes 18436
  7.2 9.7 %copy-start.5 = (bf16[8,2048]{1,0:T(8,128)(2,1)S(1)}, bf16[8,2048]{1,0:T(8,128)(2,1)}, u32[]{:S(2)}) copy-start(bf16[8,2048]{1,0:T(8,128)(2,1)} %param.16) | copy-start | bytes 98308
  7.2 9.9 %copy-start.8 = (f32[2048]{0:T(1024)S(1)}, f32[2048]{0:T(1024)}, u32[]{:S(2)}) copy-start(f32[2048]{0:T(1024)} %param.17) | copy-start | bytes 24580
  7.2 138.6 %all-reduce.3.cloned.1.call-start = ((), (), s32[]{:S(2)}) async-start(), calls=%async_computation.4 | async-start | bytes 131072 | tf_op jit(solution)/shard_map/psum | solution.py:156
  21.6 0.6 copy-start.6
  66.6 8.1 %copy-start.13 = (bf16[8,2,4,512]{3,2,1,0:T(4,128)(2,1)S(1)}, bf16[8,2,4,512]{3,2,1,0:T(4,128)(2,1)}, u32[]{:S(2)}) copy-start(bf16[8,2,4,512]{3,2,1,0:T(4,128)(2,1)} %param.22) | copy-start | bytes 196612
  100.8 11.7 %copy-start.10 = (f32[8,4]{0,1:T(4,128)S(1)}, f32[8,4]{0,1:T(4,128)}, u32[]{:S(2)}) copy-start(f32[8,4]{0,1:T(4,128)} %param.25) | copy-start | bytes 388
  100.8 11.7 %copy-start.11 = (s32[8,4]{0,1:T(4,128)S(1)}, s32[8,4]{0,1:T(4,128)}, u32[]{:S(2)}) copy-start(s32[8,4]{0,1:T(4,128)} %param.24) | copy-start | bytes 388
  110.0 67.4 %copy-start.1 = (bf16[2,256,1408]{2,1,0:T(8,128)(2,1)S(1)}, bf16[2,256,1408]{2,1,0:T(8,128)(2,1)}, u32[]{:S(2)}) copy-start(bf16[2,256,1408]{2,1,0:T(8,128)(2,1)} %param.29) | copy-start | bytes 4325380
  146.8 0.6 copy-start.4
  148.8 4.2 %collective-permute-start = (bf16[8,2048]{1,0:T(8,128)(2,1)}, bf16[8,2048]{1,0:T(8,128)(2,1)}, u32[]{:S(2)}, u32[]{:S(2)}) collective-permute-start(bf16[8,2048]{1,0:T(8,128)(2,1)} %multiply_convert_fusion), channel_id=1, source_target_pairs={{0,4},{4,0},{8,12},{12,8},{16,20},{20,16},{24,28},{28,24},{1,5},{5... | collective-permute-start | bytes 98312 | tf_op jit(solution)/shard_map/ppermute | solution.py:20
  154.5 9.3 %collective-permute-start.1 = (bf16[16,2048]{1,0:T(8,128)(2,1)}, bf16[16,2048]{1,0:T(8,128)(2,1)}, u32[]{:S(2)}, u32[]{:S(2)}) collective-permute-start(bf16[16,2048]{1,0:T(8,128)(2,1)} %maximum_select_fusion.2), channel_id=1, source_target_pairs={{0,8},{4,12},{8,0},{12,4},{16,24},{20,28},{24,16},{28,20},{1,9},{5... | collective-permute-start | bytes 196616 | tf_op jit(solution)/shard_map/ppermute | solution.py:20
  159.0 11.6 %all-to-all-start = ((bf16[8,2,2048]{2,1,0:T(2,128)(2,1)}), bf16[8,2,2048]{2,1,0:T(2,128)(2,1)}, u32[]{:S(2)}, u32[]{:S(2)}) async-start(bf16[8,2,2048]{2,1,0:T(2,128)(2,1)} %reshape.198), calls=%async_computation | async-start | bytes 131072 | tf_op jit(solution)/shard_map/all_to_all | solution.py:205
  163.6 88.9 %all-reduce.5.cloned.1.call-start = ((), (), s32[]{:S(2)}) async-start(), calls=%async_computation.5 | async-start | bytes 1441792 | tf_op jit(solution)/shard_map/psum | solution.py:166
  165.5 10.1 %collective-permute-start.2 = (bf16[32,2048]{1,0:T(8,128)(2,1)}, bf16[32,2048]{1,0:T(8,128)(2,1)}, u32[]{:S(2)}, u32[]{:S(2)}) collective-permute-start(bf16[32,2048]{1,0:T(8,128)(2,1)} %maximum_select_fusion.1), channel_id=1, source_target_pairs={{0,16},{4,20},{8,24},{12,28},{16,0},{20,4},{24,8},{28,12},{1,17},{... | collective-permute-start | bytes 393224 | tf_op jit(solution)/shard_map/ppermute | solution.py:20
  175.5 90.4 %copy-start.7 = (bf16[8,4,128]{2,0,1:T(8,128)(2,1)S(1)}, bf16[8,4,128]{2,0,1:T(8,128)(2,1)}, u32[]{:S(2)}) copy-start(bf16[8,4,128]{2,0,1:T(8,128)(2,1)} %get-tuple-element.15) | copy-start | bytes 24580
  176.7 0.7 copy-start.2
  178.6 11.7 %copy-start.3 = (bf16[64,2048]{1,0:T(8,128)(2,1)S(1)}, bf16[64,2048]{1,0:T(8,128)(2,1)}, u32[]{:S(2)}) copy-start(bf16[64,2048]{1,0:T(8,128)(2,1)} %copy-done.2) | copy-start | bytes 786436
  178.6 73.9 %copy-start.12 = (bf16[1408,256]{1,0:T(8,128)(2,1)S(1)}, bf16[1408,256]{1,0:T(8,128)(2,1)}, u32[]{:S(2)}) copy-start(bf16[1408,256]{1,0:T(8,128)(2,1)} %param.30) | copy-start | bytes 2162692
  186.7 67.2 %all-to-all-start.1 = ((f32[8,2,2048]{2,1,0:T(2,128)}), f32[8,2,2048]{2,1,0:T(2,128)S(1)}, u32[]{:S(2)}, u32[]{:S(2)}) async-start(f32[8,2,2048]{2,1,0:T(2,128)} %copy.50), calls=%async_computation.1 | async-start | bytes 262144 | tf_op jit(solution)/shard_map/all_to_all | solution.py:209
  190.3 92.1 %reduce-scatter.2.cloned.1.call-start = ((), (), s32[]{:S(2)}) async-start(), calls=%async_computation.6 | async-start | bytes 81920 | tf_op jit(solution)/shard_map/reduce_scatter | solution.py:218
Sparse Core Ops, SparseCore 0:
  112.1 33.7 all-reduce.2
  178.8 73.6 all-reduce.4
  265.4 16.9 reduce-scatter.1
